TPU v7x, 256 devices: a whole 4x4x8 slice. The times are simulated.
256 devices in a mesh: band: 8 (over z), grid: 32 (over y, x, core).
Axes of the slice: x: 4, y: 4, z: 8, core: 2. Of those that a mesh axis runs over, the one named last changes fastest.
Arguments:
- orbitals: float32 [32, 96, 9216], P('band', 'grid'), may hold values from -6 to 6
- pair_mask: int32 [32, 4], P('band'), may hold values 0 or 1
- cycle_step: int32 [], replicated, may hold values from 1 to 7
Outputs:
- exchange_field: float32 [32, 96, 9216], P('band', 'grid')
- projection: float32 [32, 4], P('band')
All inputs are finite; a program needn't handle non-finite values. No bound on the sum of `pair_mask` on one device may be relied on, other than what follows from the above.
Results may differ from a plain program's by a relative error of at most 0.0003.
Values sent between devices are 32-bit elements; how exact they have to be, the bound alone decides.
A program may use at most 64 MiB of HBM per device.

v0:
```python
import math

import jax
import jax.numpy as jnp
from jax import lax
from jax.sharding import PartitionSpec as P

NX = 96
NY = 96
NZ = 96


box_length = 16.0
highest = lax.Precision.HIGHEST


def passed_along(block, axis, distance):
    devices = range(lax.axis_size(axis))
    route = [((i - distance) % len(devices), i) for i in devices]
    return lax.ppermute(block, axis, route)


def hartley_table(length):
    index = jnp.arange(length, dtype=jnp.int32)
    product = index[:, None] * index[None, :] % length
    angle = product.astype(jnp.float32) * (2.0 * math.pi / length)
    return jnp.cos(angle) + jnp.sin(angle)


def folded(index, length):
    return jnp.where(index * 2 >= length, index - length, index).astype(jnp.float32)


def across_planes(field, table_y, table_z):
    count = field.shape[0]
    planes = field.shape[1]
    shaped = field.reshape(count * planes * NY, NZ)
    shaped = jnp.matmul(shaped, table_z, precision=highest)
    shaped = shaped.reshape(count * planes, NY, NZ)
    shaped = jnp.matmul(table_y, shaped, precision=highest)
    return shaped.reshape(count, planes, NY * NZ)


def shards(orbitals, pair_mask, cycle_step):
    orbit_count = orbitals.shape[0]
    planes = orbitals.shape[1]
    grid_count = lax.axis_size("grid")
    slab_rows = NY // grid_count

    def one_hop(turn, block):
        return passed_along(block, "band", 1)

    visiting = lax.fori_loop(0, cycle_step, one_hop, orbitals)
    table_x = hartley_table(NX)
    table_y = hartley_table(NY)
    table_z = hartley_table(NZ)
    row_index = lax.axis_index("grid") * slab_rows + jnp.arange(slab_rows, dtype=jnp.int32)
    freq_x = folded(jnp.arange(NX, dtype=jnp.int32), NX)
    freq_y = folded(row_index, NY)
    freq_z = folded(jnp.arange(NZ, dtype=jnp.int32), NZ)
    squares = freq_x[:, None, None] ** 2 + freq_y[None, :, None] ** 2 + freq_z[None, None, :] ** 2
    coulomb = box_length * box_length / math.pi / (NX * NY * NZ)
    kernel = jnp.where(squares > 0.5, coulomb / jnp.maximum(squares, 1.0), jnp.float32(0.0))
    kernel = kernel.reshape(NX, slab_rows * NZ)

    def solve_items(spectra):
        along = jnp.matmul(table_x, spectra, precision=highest) * kernel
        along = jnp.matmul(table_x, along, precision=highest)
        return lax.all_to_all(along, "grid", split_axis=1, concat_axis=2, tiled=True)

    group = orbit_count // 2
    mask_float = pair_mask.astype(jnp.float32).reshape(orbit_count // group, group, orbit_count)
    own_rows = orbitals.reshape(orbit_count // group, group, planes, NY * NZ)

    def one_group(carry, inputs):
        rows, weights = inputs
        density = (rows[:, None] * visiting[None]).reshape(group * orbit_count, planes, NY * NZ)
        spectra = across_planes(density, table_y, table_z)
        potential = solve_items(
            lax.all_to_all(spectra, "grid", split_axis=2, concat_axis=1, tiled=True)
        )
        potential = across_planes(potential, table_y, table_z)
        potential = potential.reshape(group, orbit_count, planes, NY * NZ)
        field = -jnp.einsum("aj,ajxr->axr", weights, potential * visiting[None], precision=highest)
        return (carry, field)

    start_carry = jnp.zeros((), jnp.float32)
    _, fields = lax.scan(one_group, start_carry, (own_rows, mask_float))
    exchange_field = fields.reshape(orbit_count, planes, NY * NZ)
    local_terms = jnp.einsum("axr,cxr->ac", orbitals, exchange_field, precision=highest) / (
        NX * NY * NZ
    )
    projection = lax.psum(local_terms, "grid")
    return (exchange_field, projection)


def solution(mesh):
    return jax.shard_map(
        shards,
        mesh=mesh,
        in_specs=(P("band", "grid", None), P("band", None), P()),
        out_specs=(P("band", "grid", None), P("band", None)),
        check_vma=False,
    )
```

profile of v0, /device:TPU:1, one launch (start us, length us, event | category | flops | bytes accessed | tf_op | source)
XLA Modules:
  0.0 370.3 jit_solution(11077026607436724379)
XLA Ops:
  0.6 1.0 copy.80
  1.6 30.1 %while.23 = (s32[]{:T(128)}, f32[4,3,9216]{2,0,1:T(4,128)S(1)}, s32[]{:T(128)}, s32[]{:T(128)}) while((s32[]{:T(128)}, f32[4,3,9216]{2,0,1:T(4,128)S(1)}, s32[]{:T(128)}, s32[]{:T(128)}) %tuple.51), condition=%wide.region_1.0_spmd, body=%wide.region_0.0_spmd.sunk | while | flops 2 | bytes 2654301 | solution.py:53
  2.3 2.5 collective-permute-start
  4.8 13.8 %collective-permute-done = f32[4,3,9216]{2,0,1:T(4,128)S(1)} collective-permute-done((f32[4,3,9216]{2,0,1:T(4,128)S(1)}, f32[4,3,9216]{2,0,1:T(4,128)S(1)}, u32[]{:S(2)}, u32[]{:S(2)}) %collective-permute-start) | collective-permute-done | bytes 442400 | tf_op jit(solution)/shard_map/while/body/ppermute | solution.py:20
  19.5 11.6 %collective-permute-done = f32[4,3,9216]{2,0,1:T(4,128)S(1)} collective-permute-done((f32[4,3,9216]{2,0,1:T(4,128)S(1)}, f32[4,3,9216]{2,0,1:T(4,128)S(1)}, u32[]{:S(2)}, u32[]{:S(2)}) %collective-permute-start) | collective-permute-done | bytes 442400 | tf_op jit(solution)/shard_map/while/body/ppermute | solution.py:20
  31.8 0.3 copy.44
  32.2 0.6 copy-done
  32.8 0.3 copy.43
  33.1 268.3 %while.24 = (s32[]{:T(128)}, f32[2,2,3,9216]{3,2,1,0:T(4,128)}, f32[2,2,4]{2,1,0:T(2,128)S(1)}, f32[2,2,3,9216]{3,2,1,0:T(4,128)S(1)}, f32[4,3,9216]{2,1,0:T(4,1...) while((s32[]{:T(128)}, f32[2,2,3,9216]{3,2,1,0:T(4,128)}, ...), condition=%wide.region_3.4_spmd.clone.clone, body=%wide.region_2.3_spmd.clone.clone.sunk | while | flops 1532888064 | bytes 49104724 | solution.py:88
  33.4 0.8 mul.411
  34.2 2.9 fusion.86
  37.1 1.3 convolution_bitcast_fusion.8
  38.4 0.4 copy.72
  38.8 1.0 reshape.126
  39.7 11.9 %copy.73 = f32[8,3,9216]{0,1,2:T(4,128)} copy(f32[8,3,9216]{2,1,0:T(4,128)S(1)} %reshape.126) | data formatting | bytes 1769472 | tf_op jit(solution)/shard_map/while/body/eval_jaxpr/reshape | solution.py:41
  51.6 17.9 %reshape.127 = f32[32,1,6912]{2,1,0:T(1,128)} reshape(f32[9216,3,8]{2,1,0:T(4,128)} %bitcast.120) | data formatting | bytes 1769472 | tf_op jit(solution)/shard_map/while
  69.5 9.2 %all-to-all-start = ((f32[32,1,6912]{2,1,0:T(1,128)}), f32[32,1,6912]{2,1,0:T(1,128)S(1)}, u32[]{:S(2)}, u32[]{:S(2)}) async-start(f32[32,1,6912]{2,1,0:T(1,128)} %reshape.127), calls=%async_computation | async-start | bytes 1769472 | tf_op jit(solution)/shard_map/while/body/eval_jaxpr/all_to_all | solution.py:80
  78.8 15.3 %all-to-all-done = f32[32,1,6912]{2,1,0:T(1,128)S(1)} async-done(((f32[32,1,6912]{2,1,0:T(1,128)}), f32[32,1,6912]{2,1,0:T(1,128)S(1)}, u32[]{:S(2)}, u32[]{:S(2)}) %all-to-all-start) | async-done | bytes 884768 | tf_op jit(solution)/shard_map/while/body/eval_jaxpr/all_to_all | solution.py:80
  94.1 0.5 broadcast.148
  94.6 2.7 reduce.2
  97.4 21.0 %reshape.128 = f32[9216,3,8]{2,1,0:T(4,128)} reshape(f32[32,6912]{1,0:T(8,128)S(1)} %reduce.2) | data formatting | bytes 1769472 | tf_op jit(solution)/shard_map/while
  118.4 13.8 %copy.74 = f32[8,3,32,288]{3,0,1,2:T(8,128)S(1)} copy(f32[8,3,32,288]{0,1,3,2:T(4,128)} %bitcast.121) | data formatting | bytes 1769472 | tf_op jit(solution)/shard_map/while/body/eval_jaxpr/all_to_all | solution.py:80
  132.2 2.6 fusion.88
  134.8 1.3 convolution_bitcast_fusion.9
  136.1 1.5 copy.75
  137.7 4.0 %all-to-all-start.1 = ((f32[8,96,288]{2,0,1:T(8,128)}), f32[8,96,288]{2,0,1:T(8,128)S(1)}, u32[]{:S(2)}, u32[]{:S(2)}) async-start(f32[8,96,288]{2,0,1:T(8,128)} %copy.75), calls=%async_computation.1 | async-start | bytes 2359296 | tf_op jit(solution)/shard_map/while/body/eval_jaxpr/all_to_all | solution.py:69
  141.7 17.8 %all-to-all-done.1 = f32[8,96,288]{2,0,1:T(8,128)S(1)} async-done(((f32[8,96,288]{2,0,1:T(8,128)}), f32[8,96,288]{2,0,1:T(8,128)S(1)}, u32[]{:S(2)}, u32[]{:S(2)}) %all-to-all-start.1) | async-done | bytes 884768 | tf_op jit(solution)/shard_map/while/body/eval_jaxpr/all_to_all | solution.py:69
  159.7 0.7 dot_general.51
  160.4 2.9 fusion.89
  163.4 1.3 convolution_bitcast_fusion.10
  164.7 0.4 copy.77
  165.0 1.0 reshape.129
  166.0 0.3 broadcast_multiply_fusion.5
  166.3 2.0 fusion.90
  168.5 0.8 copy-done.3
  169.5 0.8 mul.411
  170.3 2.9 fusion.86
  173.2 1.3 convolution_bitcast_fusion.8
  174.5 0.4 copy.72
  174.9 1.0 reshape.126
  175.9 11.9 %copy.73 = f32[8,3,9216]{0,1,2:T(4,128)} copy(f32[8,3,9216]{2,1,0:T(4,128)S(1)} %reshape.126) | data formatting | bytes 1769472 | tf_op jit(solution)/shard_map/while/body/eval_jaxpr/reshape | solution.py:41
  187.7 17.9 %reshape.127 = f32[32,1,6912]{2,1,0:T(1,128)} reshape(f32[9216,3,8]{2,1,0:T(4,128)} %bitcast.120) | data formatting | bytes 1769472 | tf_op jit(solution)/shard_map/while
  205.6 5.1 %all-to-all-start = ((f32[32,1,6912]{2,1,0:T(1,128)}), f32[32,1,6912]{2,1,0:T(1,128)S(1)}, u32[]{:S(2)}, u32[]{:S(2)}) async-start(f32[32,1,6912]{2,1,0:T(1,128)} %reshape.127), calls=%async_computation | async-start | bytes 1769472 | tf_op jit(solution)/shard_map/while/body/eval_jaxpr/all_to_all | solution.py:80
  210.8 15.4 %all-to-all-done = f32[32,1,6912]{2,1,0:T(1,128)S(1)} async-done(((f32[32,1,6912]{2,1,0:T(1,128)}), f32[32,1,6912]{2,1,0:T(1,128)S(1)}, u32[]{:S(2)}, u32[]{:S(2)}) %all-to-all-start) | async-done | bytes 884768 | tf_op jit(solution)/shard_map/while/body/eval_jaxpr/all_to_all | solution.py:80
  226.3 0.5 broadcast.148
  226.8 2.7 reduce.2
  229.5 21.0 %reshape.128 = f32[9216,3,8]{2,1,0:T(4,128)} reshape(f32[32,6912]{1,0:T(8,128)S(1)} %reduce.2) | data formatting | bytes 1769472 | tf_op jit(solution)/shard_map/while
  250.6 13.8 %copy.74 = f32[8,3,32,288]{3,0,1,2:T(8,128)S(1)} copy(f32[8,3,32,288]{0,1,3,2:T(4,128)} %bitcast.121) | data formatting | bytes 1769472 | tf_op jit(solution)/shard_map/while/body/eval_jaxpr/all_to_all | solution.py:80
  264.4 2.6 fusion.88
  267.0 1.3 convolution_bitcast_fusion.9
  268.3 1.5 copy.75
  269.8 4.0 %all-to-all-start.1 = ((f32[8,96,288]{2,0,1:T(8,128)}), f32[8,96,288]{2,0,1:T(8,128)S(1)}, u32[]{:S(2)}, u32[]{:S(2)}) async-start(f32[8,96,288]{2,0,1:T(8,128)} %copy.75), calls=%async_computation.1 | async-start | bytes 2359296 | tf_op jit(solution)/shard_map/while/body/eval_jaxpr/all_to_all | solution.py:69
  273.8 17.8 %all-to-all-done.1 = f32[8,96,288]{2,0,1:T(8,128)S(1)} async-done(((f32[8,96,288]{2,0,1:T(8,128)}), f32[8,96,288]{2,0,1:T(8,128)S(1)}, u32[]{:S(2)}, u32[]{:S(2)}) %all-to-all-start.1) | async-done | bytes 884768 | tf_op jit(solution)/shard_map/while/body/eval_jaxpr/all_to_all | solution.py:69
  291.8 0.7 dot_general.51
  292.6 2.9 fusion.89
  295.5 1.3 convolution_bitcast_fusion.10
  296.8 0.4 copy.77
  297.2 1.0 reshape.129
  298.4 2.0 fusion.90
  300.6 0.8 copy-done.3
  301.4 1.4 copy.52
  302.8 3.2 fusion.42
  306.0 63.6 %psum.7 = f32[4,4]{0,1:T(4,128)S(1)} all-reduce(f32[4,4]{0,1:T(4,128)S(1)} %fusion.42), channel_id=1, replica_groups=mesh['band'=8,'grid'=32] {'grid'}, use_global_device_ids=true, to_apply=%region_4.5 | all-reduce | flops 16 | bytes 128 | tf_op jit(solution)/shard_map/psum | solution.py:93
  369.6 0.7 copy.46
  (32 shorter events, 1.9 us)
Async XLA Ops:
  2.3 16.4 %collective-permute-start = (f32[4,3,9216]{2,0,1:T(4,128)S(1)}, f32[4,3,9216]{2,0,1:T(4,128)S(1)}, u32[]{:S(2)}, u32[]{:S(2)}) collective-permute-start(f32[4,3,9216]{2,0,1:T(4,128)S(1)} %get-tuple-element.255), channel_id=1, source_target_pairs={{224,0},{0,32},{32,64},{64,96},{96,128},{128,160},{160,192},{192,2... | collective-permute-start | bytes 1327112 | tf_op jit(solution)/shard_map/while/body/ppermute | solution.py:20
  19.4 11.7 %collective-permute-start = (f32[4,3,9216]{2,0,1:T(4,128)S(1)}, f32[4,3,9216]{2,0,1:T(4,128)S(1)}, u32[]{:S(2)}, u32[]{:S(2)}) collective-permute-start(f32[4,3,9216]{2,0,1:T(4,128)S(1)} %get-tuple-element.255), channel_id=1, source_target_pairs={{224,0},{0,32},{32,64},{64,96},{96,128},{128,160},{160,192},{192,2... | collective-permute-start | bytes 1327112 | tf_op jit(solution)/shard_map/while/body/ppermute | solution.py:20
  31.8 1.0 copy-start
  31.8 1.3 copy-start.4
  69.5 24.6 %all-to-all-start = ((f32[32,1,6912]{2,1,0:T(1,128)}), f32[32,1,6912]{2,1,0:T(1,128)S(1)}, u32[]{:S(2)}, u32[]{:S(2)}) async-start(f32[32,1,6912]{2,1,0:T(1,128)} %reshape.127), calls=%async_computation | async-start | bytes 1769472 | tf_op jit(solution)/shard_map/while/body/eval_jaxpr/all_to_all | solution.py:80
  137.7 21.8 %all-to-all-start.1 = ((f32[8,96,288]{2,0,1:T(8,128)}), f32[8,96,288]{2,0,1:T(8,128)S(1)}, u32[]{:S(2)}, u32[]{:S(2)}) async-start(f32[8,96,288]{2,0,1:T(8,128)} %copy.75), calls=%async_computation.1 | async-start | bytes 2359296 | tf_op jit(solution)/shard_map/while/body/eval_jaxpr/all_to_all | solution.py:69
  166.0 2.3 copy-start.2
  168.5 0.8 copy-start.3
  205.6 20.7 %all-to-all-start = ((f32[32,1,6912]{2,1,0:T(1,128)}), f32[32,1,6912]{2,1,0:T(1,128)S(1)}, u32[]{:S(2)}, u32[]{:S(2)}) async-start(f32[32,1,6912]{2,1,0:T(1,128)} %reshape.127), calls=%async_computation | async-start | bytes 1769472 | tf_op jit(solution)/shard_map/while/body/eval_jaxpr/all_to_all | solution.py:80
  269.8 21.8 %all-to-all-start.1 = ((f32[8,96,288]{2,0,1:T(8,128)}), f32[8,96,288]{2,0,1:T(8,128)S(1)}, u32[]{:S(2)}, u32[]{:S(2)}) async-start(f32[8,96,288]{2,0,1:T(8,128)} %copy.75), calls=%async_computation.1 | async-start | bytes 2359296 | tf_op jit(solution)/shard_map/while/body/eval_jaxpr/all_to_all | solution.py:69
  298.2 2.3 copy-start.2
  300.6 0.8 copy-start.3
  302.8 67.5 %copy-start.1 = (f32[4,3,9216]{2,0,1:T(4,128)}, f32[4,3,9216]{2,0,1:T(4,128)S(1)}, u32[]{:S(2)}) copy-start(f32[4,3,9216]{2,0,1:T(4,128)S(1)} %copy.52) | copy-start | bytes 1327108
where the time goes:
time: 372 us; the launch traced here: 370 us
  local copies, waits for them, and re-layouts  148 us (40%)
  waiting for transfers between devices  91.8 us (25%)
  blocking collectives  63.6 us (17%)
  matrix products  31.9 us (9%)
  starting transfers between devices  25 us (7%)
  other arithmetic  6.9 us (2%)
    while x14, local copies, waits for them, and re-layouts  79.5 us
    psum x1, blocking collectives, shards(): projection = lax.psum(local_terms, 'grid')  63.6 us
    all_to_all x2, waiting for transfers between devices, solve_items(): lax.all_to_all(along, 'grid', split_axis=1, concat_axis=2, tiled=True)  35.6 us
    all_to_all x2, waiting for transfers between devices, one_group(): lax.all_to_all(spectra, 'grid', split_axis=2, concat_axis=1, tiled=True)  30.7 us
    all_to_all x4, local copies, waits for them, and re-layouts, one_group(): lax.all_to_all(spectra, 'grid', split_axis=2, concat_axis=1, tiled=True)  28.7 us
    reshape x4, local copies, waits for them, and re-layouts, across_planes(): return shaped.reshape(count, planes, NY * NZ)  25.7 us
    ppermute x2, waiting for transfers between devices, passed_along(): return lax.ppermute(block, axis, route)  25.5 us
    all_to_all x2, starting transfers between devices, one_group(): lax.all_to_all(spectra, 'grid', split_axis=2, concat_axis=1, tiled=True)  14.4 us
  transfers between devices with their start and end apart: 6, of which 6 were waited for; matrix products, arithmetic and copies ran while one was open for 0% of the time, Pallas kernels for 0%

commit v1 on v0

v1 whole, which is shorter than its diff:
```python
import functools
import math

import jax
import jax.numpy as jnp
import numpy as np
from jax import lax
from jax.experimental import pallas as pl
from jax.experimental.pallas import tpu as pltpu
from jax.sharding import PartitionSpec as P

N = 96
LANES = 4 * N
BOX = 16.0
SIDE = 32
EACH = 3
JC = 2
CHUNKS = 4 // JC
ROWS = JC * EACH * EACH * 3
PITCH = -(-ROWS // 8) * 8
MESH = pl.DeviceIdType.MESH


def hartley():
    index = np.arange(N)
    angle = (index[:, None] * index[None, :] % N) * (2.0 * math.pi / N)
    return np.cos(angle) + np.sin(angle)


def two_parts(table):
    high = table.astype(jnp.bfloat16)
    low = (table - high.astype(np.float64)).astype(jnp.bfloat16)
    return high, low


def stacked(table):
    high, low = two_parts(table)
    return np.concatenate([np.concatenate([high, high], 1), np.concatenate([low, low], 1)], 0)


def tables():
    cas = hartley()
    order = np.array([EACH * (r % SIDE) + r // SIDE for r in range(N)])
    out_of = stacked(cas[order, :])
    into = stacked(cas[:, order])
    z_high, z_low = two_parts(np.kron(np.eye(4), cas))
    freq = np.arange(N)
    freq = np.where(freq * 2 >= N, freq - N, freq).astype(np.float32)
    squares = freq[:, None] ** 2 + np.tile(freq, 4)[None, :] ** 2
    pick = np.zeros((LANES, 128), np.float32)
    pick[np.arange(LANES), np.arange(LANES) // N] = 1.0
    return out_of, into, z_high, z_low, squares.astype(np.float32), pick.astype(jnp.bfloat16)


def split(value):
    high = value.astype(jnp.bfloat16)
    low = (value - high.astype(jnp.float32)).astype(jnp.bfloat16)
    return high, low


def dot(a, b):
    return jnp.dot(a, b, preferred_element_type=jnp.float32)


def left(table, value):
    high, low = split(value)
    both = dot(table, jnp.concatenate([high, low], 0))
    return both[:N] + both[N:]


def right(value, z_high, z_low):
    high, low = split(value)
    rows = value.shape[0]
    both = dot(jnp.concatenate([high, low], 0), z_high)
    return both[:rows] + both[rows:] + dot(high, z_low)


def one_orbital(tiles, j):
    a, b, c = tiles
    lane = lax.broadcasted_iota(jnp.int32, a.shape, 1)
    roll = lambda v, s: pltpu.roll(v, s, 1)
    if j == 0:
        v = a
    elif j == 1:
        v = jnp.where(lane < 32, roll(a, 32), roll(b, 32))
    elif j == 2:
        v = jnp.where(lane < 64, roll(b, 64), roll(c, 64))
    else:
        v = roll(c, 96)
    v32, v64, v96 = roll(v, 32), roll(v, 64), roll(v, 96)
    return [
        jnp.where(lane < 96, v, v96),
        jnp.where(lane < 64, v96, v64),
        jnp.where(lane < 32, v64, v32),
    ]


def lane_tiles(value):
    return [value[:, 128 * t : 128 * t + 128] for t in range(3)]


def body(
    own_ref, vis_ref, mask_ref, out_of_ref, into_ref, zh_ref, zl_ref, sq_ref, pick_ref,
    field_ref, proj_ref,
    rep, coulomb, send1, recv1, send2, recv2, part_send, part_recv,
    send_sem, recv_sem, own_sem, part_sems,
):
    me = lax.axis_index("grid")
    barrier = pltpu.get_barrier_semaphore()

    def greet(t, _):
        pl.semaphore_signal(barrier, inc=1, device_id={"grid": (me + t) % SIDE}, device_id_type=MESH)
        return 0

    lax.fori_loop(1, SIDE, greet, 0)

    def densities(c):
        for jj in range(JC):
            j = c * JC + jj

            def plane_step(p, _):
                vis = jnp.concatenate(one_orbital(lane_tiles(vis_ref[p]), j), 1)
                rep[j, p] = vis
                value = right(own_ref[p] * vis, zh_ref[...], zl_ref[...])
                value = left(out_of_ref[...], value)
                for k in range(EACH):
                    for b in range(3):
                        row = ((jj * EACH + p) * EACH + k) * 3 + b
                        send1[c, pl.ds(row, SIDE, stride=PITCH), :] = value[
                            k * SIDE : (k + 1) * SIDE, b * 128 : (b + 1) * 128
                        ]
                return 0

            lax.fori_loop(0, EACH, plane_step, 0)

    def exchange(way, c, send, recv):
        def one(t, _):
            to = (me + t) % SIDE
            pltpu.make_async_remote_copy(
                src_ref=send.at[c, pl.ds(pl.multiple_of(to * PITCH, 8), PITCH)],
                dst_ref=recv.at[c, pl.ds(pl.multiple_of(me * PITCH, 8), PITCH)],
                send_sem=send_sem.at[way, c],
                recv_sem=recv_sem.at[way, c],
                device_id={"grid": to},
                device_id_type=MESH,
            ).start()
            return 0

        lax.fori_loop(1, SIDE, one, 0)
        mine = pl.ds(pl.multiple_of(me * PITCH, 8), PITCH)
        pltpu.make_async_copy(send.at[c, mine], recv.at[c, mine], own_sem.at[way, c]).start()

    def arrived(way, c, send, recv):
        mine = pl.ds(pl.multiple_of(me * PITCH, 8), PITCH)
        pltpu.make_async_copy(send.at[c, mine], recv.at[c, mine], own_sem.at[way, c]).wait()
        most = pl.ds(0, (SIDE - 1) * PITCH)
        pltpu.make_async_copy(recv.at[c, most], recv.at[c, most], recv_sem.at[way, c]).wait()

    def sent(way, c, send):
        most = pl.ds(0, (SIDE - 1) * PITCH)
        pltpu.make_async_copy(send.at[c, most], send.at[c, most], send_sem.at[way, c]).wait()

    def along_x(c):
        for jj in range(JC):

            def row_step(k, _):
                def row(p, b):
                    return ((jj * EACH + p) * EACH + k) * 3 + b

                value = jnp.concatenate(
                    [
                        jnp.concatenate(
                            [recv1[c, pl.ds(row(p, b), SIDE, stride=PITCH), :] for b in range(3)], 1
                        )
                        for p in range(EACH)
                    ],
                    0,
                )
                value = left(into_ref[...], value) * coulomb[k]
                value = left(out_of_ref[...], value)
                for p in range(EACH):
                    for b in range(3):
                        send2[c, pl.ds(row(p, b), SIDE, stride=PITCH), :] = value[
                            p * SIDE : (p + 1) * SIDE, b * 128 : (b + 1) * 128
                        ]
                return 0

            lax.fori_loop(0, EACH, row_step, 0)

    def fields(c):
        for jj in range(JC):
            j = c * JC + jj

            def plane_step(p, _):
                value = jnp.concatenate(
                    [
                        jnp.concatenate(
                            [
                                recv2[
                                    c,
                                    pl.ds(((jj * EACH + p) * EACH + k) * 3 + b, SIDE, stride=PITCH),
                                    :,
                                ]
                                for b in range(3)
                            ],
                            1,
                        )
                        for k in range(EACH)
                    ],
                    0,
                )
                value = left(into_ref[...], value)
                value = right(value, zh_ref[...], zl_ref[...])
                term = value * rep[j, p] * mask_ref[pl.ds(j, 1), :]
                if j == 0:
                    field_ref[p] = -term
                else:
                    field_ref[p] = field_ref[p] - term
                return 0

            lax.fori_loop(0, EACH, plane_step, 0)

    coul = BOX * BOX / math.pi / (N * N * N)
    for k in range(EACH):
        ky = me * EACH + k
        folded = jnp.where(ky * 2 >= N, ky - N, ky).astype(jnp.float32)
        squares = sq_ref[...] + folded * folded
        coulomb[k] = jnp.where(squares > 0.5, coul / jnp.maximum(squares, 1.0), 0.0)

    densities(0)
    pl.semaphore_wait(barrier, SIDE - 1)
    exchange(0, 0, send1, recv1)
    for c in range(1, CHUNKS):
        densities(c)
        exchange(0, c, send1, recv1)
    for c in range(CHUNKS):
        arrived(0, c, send1, recv1)
        along_x(c)
        exchange(1, c, send2, recv2)
    for c in range(CHUNKS):
        arrived(1, c, send2, recv2)
        fields(c)

    rows = []
    for a in range(4):

        def plane_sum(p, total):
            own = jnp.concatenate(one_orbital(lane_tiles(own_ref[p]), a), 1)
            return total + jnp.sum(own * field_ref[p], axis=0, keepdims=True)

        rows.append(lax.fori_loop(0, EACH, plane_sum, jnp.zeros((1, LANES), jnp.float32)))
    sums = jnp.concatenate(rows + [jnp.zeros((4, LANES), jnp.float32)], 0)
    high = sums.astype(jnp.bfloat16)
    rest = sums - high.astype(jnp.float32)
    middle, low = split(rest)
    pick = pick_ref[...]
    sums = dot(high, pick) + dot(middle, pick) + dot(low, pick)
    part_send[...] = sums
    part_recv[me] = sums

    def tell(t, _):
        pltpu.make_async_remote_copy(
            src_ref=part_send,
            dst_ref=part_recv.at[me],
            send_sem=part_sems.at[0],
            recv_sem=part_sems.at[1],
            device_id={"grid": (me + t) % SIDE},
            device_id_type=MESH,
        ).start()
        return 0

    lax.fori_loop(1, SIDE, tell, 0)
    for c in range(CHUNKS):
        sent(0, c, send1)
        sent(1, c, send2)
    most = part_recv.at[pl.ds(0, SIDE - 1)]
    pltpu.make_async_copy(most, most, part_sems.at[1]).wait()
    pltpu.make_async_copy(most, most, part_sems.at[0]).wait()
    proj_ref[...] = jnp.sum(part_recv[...], axis=0) * (1.0 / (N * N * N))


def vmem(count):
    return [pl.BlockSpec(memory_space=pltpu.VMEM)] * count


def shards(orbitals, pair_mask, cycle_step):
    own = orbitals.reshape(4, EACH, N, N).transpose(1, 2, 0, 3).reshape(EACH, N, LANES)

    def moved(distance, block):
        count = lax.axis_size("band")
        return lax.ppermute(block, "band", [((i - distance) % count, i) for i in range(count)])

    visiting = lax.switch(
        cycle_step - 1, [functools.partial(moved, d) for d in range(1, 8)], own
    )
    mask = jnp.repeat(pair_mask.astype(jnp.float32).T, N, axis=1)
    buffer = pltpu.VMEM((CHUNKS, SIDE * PITCH, 128), jnp.float32)
    field, projection = pl.pallas_call(
        body,
        out_shape=(
            jax.ShapeDtypeStruct((EACH, N, LANES), jnp.float32),
            jax.ShapeDtypeStruct((8, 128), jnp.float32),
        ),
        in_specs=vmem(9),
        out_specs=tuple(vmem(2)),
        scratch_shapes=[
            pltpu.VMEM((4, EACH, N, LANES), jnp.float32),
            pltpu.VMEM((EACH, N, LANES), jnp.float32),
            buffer, buffer, buffer, buffer,
            pltpu.VMEM((8, 128), jnp.float32),
            pltpu.VMEM((SIDE, 8, 128), jnp.float32),
            pltpu.SemaphoreType.DMA((2, CHUNKS)),
            pltpu.SemaphoreType.DMA((2, CHUNKS)),
            pltpu.SemaphoreType.DMA((2, CHUNKS)),
            pltpu.SemaphoreType.DMA((2,)),
        ],
        compiler_params=pltpu.CompilerParams(
            collective_id=0, has_side_effects=True, vmem_limit_bytes=40 * 1024 * 1024
        ),
    )(own, visiting, mask, *[jnp.asarray(t) for t in tables()])
    exchange_field = field.reshape(EACH, N, 4, N).transpose(2, 0, 1, 3).reshape(4, EACH, N * N)
    return exchange_field, projection[:4, :4]


def solution(mesh):
    return jax.shard_map(
        shards,
        mesh=mesh,
        in_specs=(P("band", "grid", None), P("band", None), P()),
        out_specs=(P("band", "grid", None), P("band", None)),
        check_vma=False,
    )
```

time: 372 us -> 93.1 us (0.25)
  the two profiles are of different devices: /device:TPU:1 before, /device:TPU:33 now
where the time goes in v1:
time: 93.1 us; the launch traced here: 92.9 us
  Pallas kernels  61.3 us (66%)
  waiting for transfers between devices  21.9 us (24%)
  local copies, waits for them, and re-layouts  5.19 us (6%)
  starting transfers between devices  3.07 us (3%)
  between operations  1.4 us (2%)
    pallas_call x1, Pallas kernels, shards(): pl.pallas_call(body, out_shape=(jax.ShapeDtypeStruct((EACH, N, LANES), jn...  61.3 us
    ppermute x1, waiting for transfers between devices, moved(): lax.ppermute(block, 'band', [((i - distance) % count, i) for i in range(c...  21.9 us
    ppermute x1, starting transfers between devices, moved(): lax.ppermute(block, 'band', [((i - distance) % count, i) for i in range(c...  3.07 us
    reshape x3, local copies, waits for them, and re-layouts, shards(): orbitals.reshape(4, EACH, N, N).transpose(1, 2, 0, 3)  2.01 us
  transfers between devices with their start and end apart: 1, of which 1 were waited for; matrix products, arithmetic and copies ran while one was open for 0% of the time, Pallas kernels for 0%

profile of v1, /device:TPU:33, one launch (start us, length us, event | category | flops | bytes accessed | tf_op | source)
XLA Modules:
  0.0 92.9 jit_solution(17100436278533375589)
XLA Ops:
  1.3 0.0 copy-start.6
  1.3 0.7 copy-done.6
  2.0 0.1 copy.12
  2.1 0.1 broadcast_in_dim.3
  2.1 0.1 reshape.42.mask_ref
  2.2 1.3 %reshape.40 = f32[4,3,96,96]{3,2,0,1:T(8,128)S(1)} reshape(f32[4,3,9216]{2,0,1:T(4,128)} %param.16) | data formatting | bytes 884736 | tf_op jit(solution)/shard_map/reshape | solution.py:287
  3.6 0.4 copy.15
  3.9 0.0 copy-start
  4.0 0.0 copy-start.1
  4.0 0.0 copy-start.2
  4.0 0.0 copy-start.3
  4.0 0.0 copy-start.4
  4.0 0.0 copy-start.5
  4.0 0.3 reshape.41.own_ref
  4.3 25.0 %conditional.1 = (f32[3,96,384]{2,1,0:T(8,128)}) conditional(s32[]{:T(128)} %clamp.3, f32[3,96,384]{2,1,0:T(8,128)S(1)} %reshape.41.own_ref, f32[3,96,384]{2,1,0:T(8,128)S(1)} %reshape.41.own_ref, f32[3,96,384]{2,1,0:T(8,128)S(1)} %reshape.41.own_ref, f32[3,96,384]{2,1,0:T(8,128)S(1)} %reshape.41.own_ref, ...), branch_computations={%region_0.0_spmd, %region_1.0_spmd, %region_2.0_spmd, %region_3.0_... | conditional | bytes 1769520 | solution.py:293
  4.3 3.1 %collective-permute-start.1 = (f32[3,96,384]{2,1,0:T(8,128)S(1)}, f32[3,96,384]{2,1,0:T(8,128)}, u32[]{:S(2)}, u32[]{:S(2)}) collective-permute-start(f32[3,96,384]{2,1,0:T(8,128)S(1)} %param.1), channel_id=1, source_target_pairs={{192,0},{224,32},{0,64},{32,96},{64,128},{96,160},{128,192},{160,2... | collective-permute-start | bytes 1327112 | tf_op jit(solution)/shard_map/cond/branch_1_fun/ppermute | solution.py:291
  7.4 21.9 %collective-permute-done.1 = f32[3,96,384]{2,1,0:T(8,128)} collective-permute-done((f32[3,96,384]{2,1,0:T(8,128)S(1)}, f32[3,96,384]{2,1,0:T(8,128)}, u32[]{:S(2)}, u32[]{:S(2)}) %collective-permute-start.1) | collective-permute-done | bytes 442400 | tf_op jit(solution)/shard_map/cond/branch_1_fun/ppermute | solution.py:291
  29.3 0.0 copy-done
  29.3 0.0 copy-done.1
  29.3 0.0 copy-done.2
  29.3 0.0 copy-done.3
  29.3 0.0 copy-done.4
  29.4 0.0 copy-done.5
  29.4 61.3 %shard_map.104 = (f32[3,96,384]{2,1,0:T(8,128)S(1)}, f32[8,128]{1,0:T(8,128)S(1)}) custom-call(f32[3,96,384]{2,1,0:T(8,128)S(1)} %reshape.41.own_ref, f32[3,96,384]{2,1,0:T(8,128)} %get-tuple-element.21.vis_ref, f32[4,384]{1,0:T(4,128)S(1)} %reshape.42.mask_ref, bf16[192,192]{1,0:T(8,128)(2,1)S(1)} %copy-done.5, bf16[192,192]{1,0:T(8,128)(2,1)S(1)} %copy-done.4, ...), custom_call_target="tpu_custom_call" | custom-call | tf_op jit(solution)/shard_map/pallas_call | solution.py:298
  90.7 0.6 slice.3
  91.3 0.4 reshape.43
  91.7 1.2 %reshape.44 = f32[4,3,9216]{2,0,1:T(4,128)} reshape(f32[4,3,96,96]{3,2,0,1:T(8,128)S(1)} %copy.13) | data formatting | bytes 884736 | tf_op jit(solution)/shard_map/reshape | solution.py:321
  (2 shorter events, 0.1 us)
Async XLA Ops:
  1.3 0.7 copy-start.6
  3.9 25.4 %copy-start = (bf16[384,384]{1,0:T(8,128)(2,1)S(1)}, bf16[384,384]{1,0:T(8,128)(2,1)}, u32[]{:S(2)}) copy-start(bf16[384,384]{1,0:T(8,128)(2,1)} %constant.22.clone.zl_ref) | copy-start | bytes 884740
  4.0 25.4 %copy-start.1 = (bf16[384,384]{1,0:T(8,128)(2,1)S(1)}, bf16[384,384]{1,0:T(8,128)(2,1)}, u32[]{:S(2)}) copy-start(bf16[384,384]{1,0:T(8,128)(2,1)} %constant.21.clone.zh_ref) | copy-start | bytes 884740
  4.0 25.4 %copy-start.2 = (f32[96,384]{1,0:T(8,128)S(1)}, f32[96,384]{1,0:T(8,128)}, u32[]{:S(2)}) copy-start(f32[96,384]{1,0:T(8,128)} %constant.23.clone.sq_ref) | copy-start | bytes 442372
  4.0 25.4 %copy-start.3 = (bf16[384,128]{1,0:T(8,128)(2,1)S(1)}, bf16[384,128]{1,0:T(8,128)(2,1)}, u32[]{:S(2)}) copy-start(bf16[384,128]{1,0:T(8,128)(2,1)} %constant.24.clone.pick_ref) | copy-start | bytes 294916
  4.0 25.3 %copy-start.4 = (bf16[192,192]{1,0:T(8,128)(2,1)S(1)}, bf16[192,192]{1,0:T(8,128)(2,1)}, u32[]{:S(2)}) copy-start(bf16[192,192]{1,0:T(8,128)(2,1)} %constant.20.clone.into_ref) | copy-start | bytes 221188
  4.0 25.3 %copy-start.5 = (bf16[192,192]{1,0:T(8,128)(2,1)S(1)}, bf16[192,192]{1,0:T(8,128)(2,1)}, u32[]{:S(2)}) copy-start(bf16[192,192]{1,0:T(8,128)(2,1)} %constant.19.clone.out_of_ref) | copy-start | bytes 221188
  4.3 25.0 %collective-permute-start.1 = (f32[3,96,384]{2,1,0:T(8,128)S(1)}, f32[3,96,384]{2,1,0:T(8,128)}, u32[]{:S(2)}, u32[]{:S(2)}) collective-permute-start(f32[3,96,384]{2,1,0:T(8,128)S(1)} %param.1), channel_id=1, source_target_pairs={{192,0},{224,32},{0,64},{32,96},{64,128},{96,160},{128,192},{160,2... | collective-permute-start | bytes 1327112 | tf_op jit(solution)/shard_map/cond/branch_1_fun/ppermute | solution.py:291
